TPU v7x, 32 devices: a whole 2x2x4 slice. The times are simulated.
32 devices in a mesh: group: 4 (over y, core), depth: 8 (over z, x).
Axes of the slice: x: 2, y: 2, z: 4, core: 2. Of those that a mesh axis runs over, the one named last changes fastest.
Arguments:
- emission: bfloat16 [8, 128, 32, 1024], P('depth', 'group'), may hold values from 0.099609375 to 10
- opacity: bfloat16 [8, 128, 32, 1024], P('depth', 'group'), may hold values from 0.01 to 40
- brick_list: int32 [8, 1024, 8], P('depth', 'group'), may hold values from 0 to 127
- list_count: int32 [8, 1024], P('depth', 'group'), may hold values from 1 to 8
Outputs:
- radiance_image: float32 [1024, 128], P(('group', 'depth'))
- transmittance: float32 [1024, 128], P(('group', 'depth'))
Inputs may be any that keep to these rules, and one draw needn't show every extreme that they name: `brick_list`: entries of a list at and beyond its count are ignored.
All inputs are finite; a program needn't handle non-finite values.
Results may differ from a plain program's by a relative error of at most 0.0003.
Values may be sent and summed in bfloat16 or wider, within the bound.
A program may use at most 128 MiB of HBM per device.

v0:
```python
import jax
import jax.numpy as jnp
from jax import lax
from jax.sharding import PartitionSpec as P

RAYS = 128


EXTINCTION = 2.0


def integrate(emission, opacity, extinct_scale):
    step_depth = opacity.astype(jnp.float32) * extinct_scale
    front_depth = jnp.cumsum(step_depth, axis=-2) - step_depth
    radiance = jnp.sum(
        emission.astype(jnp.float32) * (1.0 - jnp.exp(-step_depth)) * jnp.exp(-front_depth), axis=-2
    )
    return (radiance, jnp.sum(step_depth, axis=-2))


def local(emission, opacity, brick_list, list_count):
    cell_count = emission.shape[2]
    pixel_count = emission.shape[3]
    tile_count = brick_list.shape[1]
    list_slots = brick_list.shape[2]
    sub_tiles = pixel_count // RAYS
    extinct_scale = EXTINCTION / (cell_count * list_slots * lax.axis_size("depth"))
    radiance, optical = integrate(
        lax.all_gather(emission, "group", axis=1, tiled=True)[0],
        lax.all_gather(opacity, "group", axis=1, tiled=True)[0],
        extinct_scale,
    )
    piece_rows = radiance.shape[0] * sub_tiles
    light_table = radiance.reshape(piece_rows, RAYS)
    depth_table = optical.reshape(piece_rows, RAYS)
    tile_ids = lax.axis_index("group") * tile_count + jnp.arange(tile_count, dtype=jnp.int32)
    rows_index = brick_list[0] * sub_tiles + (tile_ids % sub_tiles)[:, None]
    counts = list_count[0][:, None]
    slab_light = jnp.zeros((tile_count, RAYS), jnp.float32)
    slab_depth = jnp.zeros((tile_count, RAYS), jnp.float32)
    for slot in range(list_slots - 1, -1, -1):
        live = slot < counts
        entry_light = jnp.where(live, light_table[rows_index[:, slot]], jnp.float32(0.0))
        entry_depth = jnp.where(live, depth_table[rows_index[:, slot]], jnp.float32(0.0))
        slab_light = entry_light + jnp.exp(-entry_depth) * slab_light
        slab_depth = slab_depth + entry_depth
    slabs_light, slabs_depth = (
        lax.all_to_all(slab_light[None], "depth", split_axis=1, concat_axis=0, tiled=True),
        lax.all_to_all(slab_depth[None], "depth", split_axis=1, concat_axis=0, tiled=True),
    )
    slabs_ahead = jnp.cumsum(slabs_depth, axis=0) - slabs_depth
    radiance_image = jnp.sum(jnp.exp(-slabs_ahead) * slabs_light, axis=0)
    total_depth = jnp.sum(slabs_depth, axis=0)
    return (radiance_image, jnp.exp(-total_depth))


def solution(mesh):
    return jax.shard_map(
        local,
        mesh=mesh,
        in_specs=(
            P("depth", "group", None, None),
            P("depth", "group", None, None),
            P("depth", "group", None),
            P("depth", "group"),
        ),
        out_specs=(P(("group", "depth"), None), P(("group", "depth"), None)),
        check_vma=False,
    )
```

profile of v0, /device:TPU:0, one launch (start us, length us, event | category | flops | bytes accessed | tf_op | source)
XLA Modules:
  0.0 195.4 jit_solution(12165053263568928687)
XLA Ops:
  7.2 4.1 %copy.8 = bf16[1,32,32,1024]{3,1,2,0:T(8,128)(2,1)} copy(bf16[1,32,32,1024]{3,2,1,0:T(8,128)(2,1)} %param.5) | data formatting | bytes 4194304 | tf_op args[1]
  11.3 0.0 all-gather.5.cloned.1.call-start
  11.4 4.0 %copy.10 = bf16[1,32,32,1024]{3,1,2,0:T(8,128)(2,1)} copy(bf16[1,32,32,1024]{3,2,1,0:T(8,128)(2,1)} %param.4) | data formatting | bytes 4194304 | tf_op args[0]
  15.7 56.8 %all-gather.3.cloned.1.call-done = bf16[1,128,32,1024]{3,1,2,0:T(8,128)(2,1)} async-done(((bf16[1,32,32,1024]{3,1,2,0:T(8,128)(2,1)}), bf16[1,128,32,1024]{3,1,2,0:T(8,128)(2,1)}) %all-gather.3.cloned.1.call-update) | async-done | bytes 8388624 | tf_op jit(solution)/shard_map/all_gather | solution.py:30
  72.5 59.9 %all-gather.5.cloned.1.call-done = bf16[1,128,32,1024]{3,1,2,0:T(8,128)(2,1)} async-done(((bf16[1,32,32,1024]{3,1,2,0:T(8,128)(2,1)}), bf16[1,128,32,1024]{3,1,2,0:T(8,128)(2,1)}) %all-gather.5.cloned.1.call-update) | async-done | bytes 8388624 | tf_op jit(solution)/shard_map/all_gather | solution.py:29
  132.3 13.6 %fusion.1 = f32[128,1024]{1,0:T(8,128)S(1)} fusion(bf16[1,128,32,1024]{3,1,2,0:T(8,128)(2,1)} %all-gather.3.cloned.1.call-done, bf16[1,128,32,1024]{3,1,2,0:T(8,128)(2,1)} %all-gather.5.cloned.1.call-done), kind=kOutput, calls=%fused_computation.18 | output fusion | flops 180224000 | bytes 17301504 | tf_op jit(solution)/shard_map/jit(cumsum)/reduce_window_sum | solution.py:14
  146.0 0.1 reshape.831
  146.0 0.7 gather_fusion.15
  146.8 0.7 gather_fusion.14
  147.5 5.5 %fusion.8 = f32[128,1024]{1,0:T(8,128)S(1)} fusion(bf16[1,128,32,1024]{3,1,2,0:T(8,128)(2,1)} %all-gather.3.cloned.1.call-done), kind=kLoop, calls=%fused_computation.28 | loop fusion | flops 12451840 | bytes 8912896 | tf_op jit(solution)/shard_map/reduce_sum | solution.py:18
  153.0 0.1 reshape.830
  153.1 0.7 gather_fusion
  153.8 0.7 gather_fusion.1
  154.5 0.7 gather_fusion.13
  155.3 0.7 gather_fusion.2
  156.0 0.7 gather_fusion.12
  156.7 0.7 gather_fusion.3
  157.5 0.7 gather_fusion.11
  158.2 0.7 gather_fusion.4
  158.9 0.7 gather_fusion.10
  159.7 0.7 gather_fusion.5
  160.4 0.7 gather_fusion.9
  161.1 0.7 gather_fusion.6
  161.8 0.7 gather_fusion.8
  162.6 0.7 gather_fusion.7
  163.3 1.2 fusion.27
  164.5 5.5 %all-to-all-start.1 = ((f32[1,256,128]{2,0,1:T(1,128)}), f32[1,256,128]{2,0,1:T(1,128)S(1)}, u32[]{:S(2)}, u32[]{:S(2)}) async-start(f32[1,256,128]{2,0,1:T(1,128)} %bitcast.29), calls=%async_computation.1 | async-start | bytes 262144 | tf_op jit(solution)/shard_map/all_to_all | solution.py:48
  170.0 0.3 add_add_fusion
  170.4 7.1 %all-to-all-done.1 = f32[1,256,128]{2,0,1:T(1,128)S(1)} async-done(((f32[1,256,128]{2,0,1:T(1,128)}), f32[1,256,128]{2,0,1:T(1,128)S(1)}, u32[]{:S(2)}, u32[]{:S(2)}) %all-to-all-start.1) | async-done | bytes 131104 | tf_op jit(solution)/shard_map/all_to_all | solution.py:48
  177.4 9.8 %all_to_all.24 = f32[1,256,128]{2,0,1:T(1,128)S(1)} all-to-all(f32[1,256,128]{2,0,1:T(1,128)S(1)} %bitcast.148), channel_id=1, replica_groups=mesh['group'=4,'depth'=8] {'depth'}, dimensions={1} | all-to-all | bytes 262144 | tf_op jit(solution)/shard_map/all_to_all | solution.py:49
  187.3 0.6 fusion.30
  187.9 0.6 negate_exponential_fusion
  (20 shorter events, 0.2 us)
Async XLA Ops:
  7.2 8.3 %copy-start = (s32[1,256,8]{1,2,0:T(8,128)S(1)}, s32[1,256,8]{1,2,0:T(8,128)}, u32[]{:S(2)}) copy-start(s32[1,256,8]{1,2,0:T(8,128)} %param.6) | copy-start | bytes 24580
  7.2 8.5 %copy-start.1 = (s32[1,256]{1,0:T(1,128)S(1)}, s32[1,256]{1,0:T(1,128)}, u32[]{:S(2)}) copy-start(s32[1,256]{1,0:T(1,128)} %param.7) | copy-start | bytes 3076
  7.2 65.3 %all-gather.3.cloned.1.call-start = ((), (), s32[]{:S(2)}) async-start(), calls=%async_computation.2 | async-start | bytes 10485760 | tf_op jit(solution)/shard_map/all_gather | solution.py:30
  11.3 121.0 %all-gather.5.cloned.1.call-start = ((), (), s32[]{:S(2)}) async-start(), calls=%async_computation.3 | async-start | bytes 10485760 | tf_op jit(solution)/shard_map/all_gather | solution.py:29
  164.5 12.9 %all-to-all-start.1 = ((f32[1,256,128]{2,0,1:T(1,128)}), f32[1,256,128]{2,0,1:T(1,128)S(1)}, u32[]{:S(2)}, u32[]{:S(2)}) async-start(f32[1,256,128]{2,0,1:T(1,128)} %bitcast.29), calls=%async_computation.1 | async-start | bytes 262144 | tf_op jit(solution)/shard_map/all_to_all | solution.py:48
Sparse Core Ops, SparseCore 0:
  11.5 60.9 all-gather.2
  74.1 58.2 all-gather.4
where the time goes:
time: 196 us; the launch traced here: 195 us
  waiting for transfers between devices  124 us (63%)
  other arithmetic  22 us (11%)
  local copies, waits for them, and re-layouts  20 us (10%)
  between operations  14.2 us (7%)
  blocking collectives  9.84 us (5%)
  starting transfers between devices  5.6 us (3%)
    all_gather x1, waiting for transfers between devices, local(): lax.all_gather(emission, 'group', axis=1, tiled=True)[0]  59.9 us
    all_gather x1, waiting for transfers between devices, local(): lax.all_gather(opacity, 'group', axis=1, tiled=True)[0]  56.8 us
    another operation x1, other arithmetic, integrate(): front_depth = jnp.cumsum(step_depth, axis=-2) - step_depth  13.6 us
    all_to_all x1, blocking collectives, local(): lax.all_to_all(slab_depth[None], 'depth', split_axis=1, concat_axis=0, ti...  9.84 us
    unnamed x6, local copies, waits for them, and re-layouts  8.14 us
    all_to_all x1, waiting for transfers between devices, local(): lax.all_to_all(slab_light[None], 'depth', split_axis=1, concat_axis=0, ti...  7.06 us
    gather x8, local copies, waits for them, and re-layouts, local(): light_table[rows_index[:, slot]]  5.83 us
    gather x8, local copies, waits for them, and re-layouts, local(): depth_table[rows_index[:, slot]]  5.83 us
  transfers between devices with their start and end apart: 3, of which 3 were waited for; matrix products, arithmetic and copies ran while one was open for 2% of the time, Pallas kernels for 0%

commit v1 on v0

v1 whole, which is shorter than its diff:
```python
import functools
import math

import jax
import jax.numpy as jnp
from jax import lax
from jax.experimental import pallas as pl
from jax.experimental.pallas import tpu as pltpu
from jax.sharding import PartitionSpec as P

RAYS = 128
EXTINCTION = 2.0
MESH = pl.DeviceIdType.MESH
ROWS = 8


def peer_order(n):
    if n % 2:
        return [(0, k) for k in range(1, n)] + [(0, 0)], 1, n
    chips = n // 2
    far = sorted(range(chips), key=lambda k: -min(k, chips - k))
    return [(dy, dc) for dy in far for dc in ((1, 0) if dy == 0 else (0, 1))], chips, 2


def kernel(
    n_group,
    n_depth,
    cells,
    slots,
    bricks,
    pixels,
    tiles,
    emission,
    opacity,
    brick_list,
    counts,
    image_out,
    trans_out,
    emit_buf,
    opac_buf,
    piece,
    table,
    list_rows,
    list_cols,
    slab_buf,
    recv_buf,
    final,
    emit_sem,
    opac_sem,
    piece_send,
    piece_recv,
    list_send,
    list_recv,
    slab_send,
    slab_recv,
):
    my_group = lax.axis_index("group")
    my_depth = lax.axis_index("depth")
    sub = pixels // RAYS
    share = pixels // n_group
    classes = share // RAYS
    own = tiles // n_depth
    steps = own // sub
    rows = classes * steps
    total_bricks = bricks * n_group
    scale = EXTINCTION / (cells * slots * n_depth)

    offsets, chips, cores = peer_order(n_group)
    my_chip, my_core = my_group // cores, my_group % cores
    order = [lax.rem(my_chip + dy, chips) * cores + lax.rem(my_core + dc, cores) for dy, dc in offsets]

    loads = []
    for at, peer in enumerate(order):
        lanes = pl.ds(pl.multiple_of(peer * share, RAYS), share)
        loads.append(
            (
                pltpu.make_async_copy(emission.at[0, :, :, lanes], emit_buf.at[at], emit_sem.at[at]),
                pltpu.make_async_copy(opacity.at[0, :, :, lanes], opac_buf.at[at], opac_sem.at[at]),
            )
        )
    for pair in loads:
        pair[1].start()
        pair[0].start()

    barrier = pltpu.get_barrier_semaphore()

    @pl.loop(1, n_group * n_depth)
    def _(shift):
        to = lax.rem(my_group * n_depth + my_depth + shift, n_group * n_depth)
        pl.semaphore_signal(
            barrier, inc=1, device_id=(to // n_depth, lax.rem(to, n_depth)), device_id_type=MESH
        )

    slot_ids = lax.broadcasted_iota(jnp.int32, (slots, tiles), 0)
    flipped = jnp.transpose(brick_list[0].astype(jnp.float32))
    list_rows[my_group] = jnp.where(slot_ids < counts[...], flipped, -1.0)

    height = ROWS * cells
    row = lax.broadcasted_iota(jnp.int32, (height, height), 0)
    column = lax.broadcasted_iota(jnp.int32, (height, height), 1)
    cell = row // ROWS
    gap = column - (row - cell * ROWS) * cells
    move = jnp.where(gap == cell, 1.0, 0.0).astype(jnp.bfloat16)
    running = jnp.where((gap >= 0) & (gap <= cell), 1.0, 0.0).astype(jnp.bfloat16)

    pl.semaphore_wait(barrier, n_group * n_depth - 1)

    list_copies = []
    for at in range(n_group - 1):
        list_copies.append(
            pltpu.make_async_remote_copy(
                src_ref=list_rows.at[my_group],
                dst_ref=list_rows.at[my_group],
                send_sem=list_send.at[at],
                recv_sem=list_recv.at[my_group],
                device_id=(order[at], my_depth),
                device_id_type=MESH,
            )
        )
        list_copies[-1].start()

    def integrate(at, first):
        opac = opac_buf[at, pl.ds(first, ROWS)].reshape(height, share)
        emit = emit_buf[at, pl.ds(first, ROWS)].reshape(height, share)
        depth = jnp.dot(running, opac, preferred_element_type=jnp.float32)
        source = jnp.dot(move, emit, preferred_element_type=jnp.float32)
        before = jnp.ones((ROWS, share), jnp.float32)
        light = jnp.zeros((ROWS, share), jnp.float32)
        for k in range(cells):
            after = jnp.exp2(depth[k * ROWS : (k + 1) * ROWS] * (-scale * math.log2(math.e)))
            light = light + source[k * ROWS : (k + 1) * ROWS] * (before - after)
            before = after
        return light, depth[(cells - 1) * ROWS :] * scale

    piece_copies = []
    for at, peer in enumerate(order):
        loads[at][1].wait()
        loads[at][0].wait()

        @pl.loop(0, bricks // (2 * ROWS))
        def _(block):
            first = pl.multiple_of(block * 2 * ROWS, 2 * ROWS)
            parts = [integrate(at, first), integrate(at, first + ROWS)]
            for value in range(2):
                whole = jnp.concatenate([parts[0][value], parts[1][value]], axis=0)
                high = whole.astype(jnp.bfloat16)
                low = (whole - high.astype(jnp.float32)).astype(jnp.bfloat16)
                for c in range(classes):
                    lanes = slice(c * RAYS, (c + 1) * RAYS)
                    at_lanes = pl.ds(value * RAYS, RAYS)
                    piece[at, c, 0, pl.ds(first, 2 * ROWS), at_lanes] = high[:, lanes]
                    piece[at, c, 1, pl.ds(first, 2 * ROWS), at_lanes] = low[:, lanes]

        mine = pl.ds(pl.multiple_of(my_group * bricks, 2 * ROWS), bricks)
        if at < n_group - 1:
            copy = pltpu.make_async_remote_copy(
                src_ref=piece.at[at],
                dst_ref=table.at[:, :, mine, :],
                send_sem=piece_send.at[at],
                recv_sem=piece_recv.at[my_group],
                device_id=(peer, my_depth),
                device_id_type=MESH,
            )
            copy.start()
            piece_copies.append(copy)
        else:
            table[:, :, mine, :] = piece[at]

    for at in range(n_group - 1):
        list_copies[at].wait_send()
        pltpu.make_async_remote_copy(
            src_ref=list_rows.at[order[at]],
            dst_ref=list_rows.at[order[at]],
            send_sem=list_send.at[at],
            recv_sem=list_recv.at[order[at]],
            device_id=(order[at], my_depth),
            device_id_type=MESH,
        ).wait_recv()
    for s in range(n_group):
        list_cols[s] = jnp.transpose(jnp.concatenate([list_rows[s]] * (RAYS // slots), axis=0))

    for at in range(n_group - 1):
        piece_copies[at].wait_send()
        theirs = pl.ds(pl.multiple_of(order[at] * bricks, 2 * ROWS), bricks)
        pltpu.make_async_remote_copy(
            src_ref=piece.at[at],
            dst_ref=table.at[:, :, theirs, :],
            send_sem=piece_send.at[at],
            recv_sem=piece_recv.at[order[at]],
            device_id=(order[at], my_depth),
            device_id_type=MESH,
        ).wait_recv()

    count = steps * n_depth
    brick_ids = lax.broadcasted_iota(jnp.int32, (count, total_bricks), 1).astype(jnp.float32)

    def slab_copy(s, d):
        return pltpu.make_async_remote_copy(
            src_ref=slab_buf.at[s, d],
            dst_ref=recv_buf.at[my_depth, my_group],
            send_sem=slab_send.at[s, d],
            recv_sem=slab_recv.at[my_depth, my_group],
            device_id=(s, d),
            device_id_type=MESH,
        )

    for s in order:
        for c in range(classes):
            mark = my_group * classes + c
            entries = jnp.concatenate(
                [list_cols[s, pl.ds(mark + sub * i, n_depth, stride=own), :] for i in range(steps)], axis=0
            )
            picks = [
                jnp.where(entries[:, l : l + 1] == brick_ids, 1.0, 0.0).astype(jnp.bfloat16) for l in range(slots)
            ]
            picks = jnp.concatenate(picks, axis=0)
            picks = jnp.concatenate([picks, picks], axis=1)
            found = jnp.dot(
                picks, table[c].reshape(2 * total_bricks, 2 * RAYS), preferred_element_type=jnp.float32
            )
            light = jnp.zeros((count, RAYS), jnp.float32)
            depth = jnp.zeros((count, RAYS), jnp.float32)
            for l in range(slots - 1, -1, -1):
                entry_light = found[l * count : (l + 1) * count, :RAYS]
                entry_depth = found[l * count : (l + 1) * count, RAYS:]
                light = entry_light + jnp.exp(-entry_depth) * light
                depth = depth + entry_depth
            for value, data in enumerate((light, depth)):
                for i in range(steps):
                    slab_buf[s, :, value * rows + c * steps + i, :] = data[i * n_depth : (i + 1) * n_depth]

        @pl.loop(0, n_depth)
        def _(d):
            @pl.when(jnp.logical_or(s != my_group, d != my_depth))
            def _():
                slab_copy(s, d).start()

    recv_buf[my_depth, my_group] = slab_buf[my_group, my_depth]

    @pl.loop(0, n_group * n_depth)
    def _(which):
        g, d = which // n_depth, lax.rem(which, n_depth)

        @pl.when(jnp.logical_or(g != my_group, d != my_depth))
        def _():
            slab_copy(g, d).wait_send()
            pltpu.make_async_remote_copy(
                src_ref=slab_buf.at[g, d],
                dst_ref=recv_buf.at[d, g],
                send_sem=slab_send.at[g, d],
                recv_sem=slab_recv.at[d, g],
                device_id=(g, d),
                device_id_type=MESH,
            ).wait_recv()

    light = jnp.zeros((n_group, rows, RAYS), jnp.float32)
    depth = jnp.zeros((n_group, rows, RAYS), jnp.float32)
    for d in range(n_depth - 1, -1, -1):
        slab_light = recv_buf[d, :, :rows, :]
        slab_depth = recv_buf[d, :, rows:, :]
        light = slab_light + jnp.exp(-slab_depth) * light
        depth = depth + slab_depth
    for g in range(n_group):
        final[0, g * rows : (g + 1) * rows, :] = light[g]
        final[1, g * rows : (g + 1) * rows, :] = jnp.exp(-depth[g])
    for i in range(steps):
        image_out[i * sub : (i + 1) * sub, :] = final[0, pl.ds(i, sub, stride=steps), :]
        trans_out[i * sub : (i + 1) * sub, :] = final[1, pl.ds(i, sub, stride=steps), :]


def local(emission, opacity, brick_list, list_count):
    n_group, n_depth = lax.axis_size("group"), lax.axis_size("depth")
    _, bricks, cells, pixels = emission.shape
    _, tiles, slots = brick_list.shape
    share = pixels // n_group
    classes = share // RAYS
    own = tiles // n_depth
    rows = classes * own // (pixels // RAYS)
    any_space = pl.BlockSpec(memory_space=pl.ANY)
    in_vmem = pl.BlockSpec(memory_space=pltpu.VMEM)
    dma = pltpu.SemaphoreType.DMA
    image, trans = pl.pallas_call(
        functools.partial(kernel, n_group, n_depth, cells, slots, bricks, pixels, tiles),
        out_shape=[jax.ShapeDtypeStruct((own, RAYS), jnp.float32)] * 2,
        in_specs=[any_space, any_space, in_vmem, in_vmem],
        out_specs=[in_vmem, in_vmem],
        scratch_shapes=[
            pltpu.VMEM((n_group, bricks, cells, share), jnp.bfloat16),
            pltpu.VMEM((n_group, bricks, cells, share), jnp.bfloat16),
            pltpu.VMEM((n_group, classes, 2, bricks, 2 * RAYS), jnp.bfloat16),
            pltpu.VMEM((classes, 2, bricks * n_group, 2 * RAYS), jnp.bfloat16),
            pltpu.VMEM((n_group, slots, tiles), jnp.float32),
            pltpu.VMEM((n_group, tiles, RAYS), jnp.float32),
            pltpu.VMEM((n_group, n_depth, 2 * rows, RAYS), jnp.float32),
            pltpu.VMEM((n_depth, n_group, 2 * rows, RAYS), jnp.float32),
            pltpu.VMEM((2, n_group * rows, RAYS), jnp.float32),
            dma((n_group,)),
            dma((n_group,)),
            dma((n_group,)),
            dma((n_group,)),
            dma((n_group,)),
            dma((n_group,)),
            dma((n_group, n_depth)),
            dma((n_depth, n_group)),
        ],
        compiler_params=pltpu.CompilerParams(
            collective_id=0, has_side_effects=True, vmem_limit_bytes=48 * 1024 * 1024
        ),
    )(emission, opacity, brick_list, list_count)
    return image, trans


def solution(mesh):
    return jax.shard_map(
        local,
        mesh=mesh,
        in_specs=(
            P("depth", "group", None, None),
            P("depth", "group", None, None),
            P("depth", "group", None),
            P("depth", "group"),
        ),
        out_specs=(P(("group", "depth"), None), P(("group", "depth"), None)),
        check_vma=False,
    )
```

time: 196 us -> 27.9 us (0.14)
  waiting for transfers between devices: 124 us -> 0 us
  other arithmetic: 22 us -> 0 us
  Pallas kernels: 0 us -> 21.1 us
  local copies, waits for them, and re-layouts: 20 us -> 5.89 us
  between operations: 14.2 us -> 0.66 us
  blocking collectives: 9.84 us -> 0 us
  starting transfers between devices: 5.6 us -> 0 us
    all_gather x2 -> x0, waiting for transfers between devices: 117 us -> none  [the longest x1 59.9 us: local(): lax.all_gather(emission, 'group', axis=1, tiled=True)[0]]
    pallas_call x0 -> x1, Pallas kernels: none -> 21.1 us  [local(): pl.pallas_call(functools.partial(kernel, n_group, n_depth, cells, slots,...]
    another operation x2 -> x0, other arithmetic: 14.2 us -> none  [the longest x1 13.6 us: integrate(): front_depth = jnp.cumsum(step_depth, axis=-2) - step_depth]
    gather x16 -> x0, local copies, waits for them, and re-layouts: 11.7 us -> none  [the longest x8 5.83 us: local(): light_table[rows_index[:, slot]]]
    all_to_all x1 -> x0, blocking collectives: 9.84 us -> none  [local(): lax.all_to_all(slab_depth[None], 'depth', split_axis=1, concat_axis=0, ti...]
    all_to_all x1 -> x0, waiting for transfers between devices: 7.06 us -> none  [local(): lax.all_to_all(slab_light[None], 'depth', split_axis=1, concat_axis=0, ti...]
    all_to_all x1 -> x0, starting transfers between devices: 5.52 us -> none  [local(): lax.all_to_all(slab_light[None], 'depth', split_axis=1, concat_axis=0, ti...]
    reduce_sum x2 -> x0, other arithmetic: 5.5 us -> none  [the longest x1 5.48 us: integrate(): return (radiance, jnp.sum(step_depth, axis=-2))]
  transfers between devices with their start and end apart: 3 -> 0, of which waited for: 3 -> 0; matrix products, arithmetic and copies ran while one was open for 2% -> 0% of each run, Pallas kernels for 0% -> 0%
where the time goes in v1:
time: 27.9 us; the launch traced here: 27.6 us
  Pallas kernels  21.1 us (76%)
  local copies, waits for them, and re-layouts  5.89 us (21%)
  between operations  0.66 us (2%)
    pallas_call x1, Pallas kernels, local(): pl.pallas_call(functools.partial(kernel, n_group, n_depth, cells, slots,...  21.1 us
    unnamed x9, local copies, waits for them, and re-layouts  5.89 us

profile of v1, /device:TPU:0, one launch (start us, length us, event | category | flops | bytes accessed | tf_op | source)
XLA Modules:
  0.0 27.6 jit_solution(7374187620510887107)
XLA Ops:
  0.6 0.8 %copy.6.brick_list = s32[1,256,8]{2,1,0:T(8,128)S(1)} copy(s32[1,256,8]{1,2,0:T(8,128)} %param.6) | data formatting | bytes 16384 | tf_op args[2]
  1.5 0.0 copy-start
  1.5 1.6 %copy-done = bf16[1,32,32,1024]{3,2,1,0:T(8,128)(2,1)S(1)} copy-done((bf16[1,32,32,1024]{3,2,1,0:T(8,128)(2,1)S(1)}, bf16[1,32,32,1024]{3,2,1,0:T(8,128)(2,1)}, u32[]{:S(2)}) %copy-start) | copy-done | bytes 2097176
  3.1 0.0 copy-start.1
  3.1 1.6 %copy-done.1 = bf16[1,32,32,1024]{3,2,1,0:T(8,128)(2,1)S(1)} copy-done((bf16[1,32,32,1024]{3,2,1,0:T(8,128)(2,1)S(1)}, bf16[1,32,32,1024]{3,2,1,0:T(8,128)(2,1)}, u32[]{:S(2)}) %copy-start.1) | copy-done | bytes 2097176
  4.6 0.0 copy-start.2
  4.6 0.7 %copy-done.2 = s32[1,256]{1,0:T(1,128)S(1)} copy-done((s32[1,256]{1,0:T(1,128)S(1)}, s32[1,256]{1,0:T(1,128)}, u32[]{:S(2)}) %copy-start.2) | copy-done | bytes 1048
  5.3 21.1 %shard_map.59 = (f32[32,128]{1,0:T(8,128)S(1)}, f32[32,128]{1,0:T(8,128)S(1)}) custom-call(bf16[1,32,32,1024]{3,2,1,0:T(8,128)(2,1)S(1)} %copy-done, bf16[1,32,32,1024]{3,2,1,0:T(8,128)(2,1)S(1)} %copy-done.1, s32[1,256,8]{2,1,0:T(8,128)S(1)} %copy.6.brick_list, s32[1,256]{1,0:T(1,128)S(1)} %copy-done.2), custom_call_target="tpu_custom_call" | custom-call | tf_op jit(solution)/shard_map/pallas_call | solution.py:282
  26.4 0.6 %copy.9 = f32[32,128]{1,0:T(8,128)} copy(f32[32,128]{1,0:T(8,128)S(1)} %get-tuple-element.4) | data formatting | bytes 32768
  27.0 0.6 %copy.10 = f32[32,128]{1,0:T(8,128)} copy(f32[32,128]{1,0:T(8,128)S(1)} %get-tuple-element.5) | data formatting | bytes 32768
Async XLA Ops:
  1.5 1.6 %copy-start = (bf16[1,32,32,1024]{3,2,1,0:T(8,128)(2,1)S(1)}, bf16[1,32,32,1024]{3,2,1,0:T(8,128)(2,1)}, u32[]{:S(2)}) copy-start(bf16[1,32,32,1024]{3,2,1,0:T(8,128)(2,1)} %emission.1) | copy-start | bytes 6291460
  3.1 1.6 %copy-start.1 = (bf16[1,32,32,1024]{3,2,1,0:T(8,128)(2,1)S(1)}, bf16[1,32,32,1024]{3,2,1,0:T(8,128)(2,1)}, u32[]{:S(2)}) copy-start(bf16[1,32,32,1024]{3,2,1,0:T(8,128)(2,1)} %opacity.1) | copy-start | bytes 6291460
  4.6 0.7 %copy-start.2 = (s32[1,256]{1,0:T(1,128)S(1)}, s32[1,256]{1,0:T(1,128)}, u32[]{:S(2)}) copy-start(s32[1,256]{1,0:T(1,128)} %counts.1) | copy-start | bytes 3076

commit v2 on v1

--- a/solution.py
+++ b/solution.py
@@ -45,6 +45,9 @@
     slab_buf,
     recv_buf,
     final,
+    list_in,
+    count_row,
+    small_sem,
     emit_sem,
     opac_sem,
     piece_send,
@@ -69,6 +72,12 @@
     my_chip, my_core = my_group // cores, my_group % cores
     order = [lax.rem(my_chip + dy, chips) * cores + lax.rem(my_core + dc, cores) for dy, dc in offsets]
 
+    small = (
+        pltpu.make_async_copy(brick_list.at[0], list_in, small_sem.at[0]),
+        pltpu.make_async_copy(counts, count_row, small_sem.at[1]),
+    )
+    for load in small:
+        load.start()
     loads = []
     for at, peer in enumerate(order):
         lanes = pl.ds(pl.multiple_of(peer * share, RAYS), share)
@@ -92,8 +101,9 @@
         )
 
     slot_ids = lax.broadcasted_iota(jnp.int32, (slots, tiles), 0)
-    flipped = jnp.transpose(brick_list[0].astype(jnp.float32))
-    list_rows[my_group] = jnp.where(slot_ids < counts[...], flipped, -1.0)
+    for load in small:
+        load.wait()
+    list_rows[my_group] = jnp.where(slot_ids < count_row[...], list_in[...].astype(jnp.float32), -1.0)
 
     height = ROWS * cells
     row = lax.broadcasted_iota(jnp.int32, (height, height), 0)
@@ -276,13 +286,13 @@
     classes = share // RAYS
     own = tiles // n_depth
     rows = classes * own // (pixels // RAYS)
-    any_space = pl.BlockSpec(memory_space=pl.ANY)
+    in_hbm = pl.BlockSpec(memory_space=pltpu.HBM)
     in_vmem = pl.BlockSpec(memory_space=pltpu.VMEM)
     dma = pltpu.SemaphoreType.DMA
     image, trans = pl.pallas_call(
         functools.partial(kernel, n_group, n_depth, cells, slots, bricks, pixels, tiles),
         out_shape=[jax.ShapeDtypeStruct((own, RAYS), jnp.float32)] * 2,
-        in_specs=[any_space, any_space, in_vmem, in_vmem],
+        in_specs=[in_hbm] * 4,
         out_specs=[in_vmem, in_vmem],
         scratch_shapes=[
             pltpu.VMEM((n_group, bricks, cells, share), jnp.bfloat16),
@@ -294,6 +304,9 @@
             pltpu.VMEM((n_group, n_depth, 2 * rows, RAYS), jnp.float32),
             pltpu.VMEM((n_depth, n_group, 2 * rows, RAYS), jnp.float32),
             pltpu.VMEM((2, n_group * rows, RAYS), jnp.float32),
+            pltpu.VMEM((slots, tiles), jnp.int32),
+            pltpu.VMEM((1, tiles), jnp.int32),
+            dma((2,)),
             dma((n_group,)),
             dma((n_group,)),
             dma((n_group,)),
@@ -304,9 +317,9 @@
             dma((n_depth, n_group)),
         ],
         compiler_params=pltpu.CompilerParams(
-            collective_id=0, has_side_effects=True, vmem_limit_bytes=48 * 1024 * 1024
+            collective_id=0, has_side_effects=True, vmem_limit_bytes=60 * 1024 * 1024
         ),
-    )(emission, opacity, brick_list, list_count)
+    )(emission, opacity, jnp.swapaxes(brick_list, 1, 2), list_count)
     return image, trans
 
 

time: 27.9 us -> 24.9 us (0.89)
  local copies, waits for them, and re-layouts: 5.89 us -> 2.65 us
    unnamed x9 -> x2, local copies, waits for them, and re-layouts: 5.89 us -> 2.65 us
where the time goes in v2:
time: 24.9 us; the launch traced here: 24.6 us
  Pallas kernels  21.3 us (86%)
  local copies, waits for them, and re-layouts  2.65 us (11%)
  between operations  0.64 us (3%)
    pallas_call x1, Pallas kernels, local(): pl.pallas_call(functools.partial(kernel, n_group, n_depth, cells, slots,...  21.3 us
    unnamed x2, local copies, waits for them, and re-layouts  2.65 us

profile of v2, /device:TPU:0, one launch (start us, length us, event | category | flops | bytes accessed | tf_op | source)
XLA Modules:
  0.0 24.6 jit_solution(8428037802694862719)
XLA Ops:
  0.6 21.3 %shard_map.59 = (f32[32,128]{1,0:T(8,128)}, f32[32,128]{1,0:T(8,128)}) custom-call(bf16[1,32,32,1024]{3,2,1,0:T(8,128)(2,1)} %emission.1, bf16[1,32,32,1024]{3,2,1,0:T(8,128)(2,1)} %opacity.1, s32[1,8,256]{2,1,0:T(8,128)} %bitcast.1, s32[1,256]{1,0:T(1,128)} %counts.1), custom_call_target="tpu_custom_call" | custom-call | tf_op jit(solution)/shard_map/pallas_call | solution.py:292
  21.9 1.3 %copy.8 = f32[32,128]{1,0:T(8,128)} copy(f32[32,128]{1,0:T(8,128)} %get-tuple-element.4) | data formatting | bytes 32768
  23.3 1.3 %copy.9 = f32[32,128]{1,0:T(8,128)} copy(f32[32,128]{1,0:T(8,128)} %get-tuple-element.5) | data formatting | bytes 32768

commit v3 on v2

--- a/solution.py
+++ b/solution.py
@@ -11,6 +11,7 @@
 RAYS = 128
 EXTINCTION = 2.0
 MESH = pl.DeviceIdType.MESH
+BEFORE = 1
 ROWS = 8
 
 
@@ -35,7 +36,6 @@
     brick_list,
     counts,
     image_out,
-    trans_out,
     emit_buf,
     opac_buf,
     piece,
@@ -113,21 +113,22 @@
     move = jnp.where(gap == cell, 1.0, 0.0).astype(jnp.bfloat16)
     running = jnp.where((gap >= 0) & (gap <= cell), 1.0, 0.0).astype(jnp.bfloat16)
 
-    pl.semaphore_wait(barrier, n_group * n_depth - 1)
-
     list_copies = []
-    for at in range(n_group - 1):
-        list_copies.append(
-            pltpu.make_async_remote_copy(
-                src_ref=list_rows.at[my_group],
-                dst_ref=list_rows.at[my_group],
-                send_sem=list_send.at[at],
-                recv_sem=list_recv.at[my_group],
-                device_id=(order[at], my_depth),
-                device_id_type=MESH,
+
+    def enter():
+        pl.semaphore_wait(barrier, n_group * n_depth - 1)
+        for at in range(n_group - 1):
+            list_copies.append(
+                pltpu.make_async_remote_copy(
+                    src_ref=list_rows.at[my_group],
+                    dst_ref=list_rows.at[my_group],
+                    send_sem=list_send.at[at],
+                    recv_sem=list_recv.at[my_group],
+                    device_id=(order[at], my_depth),
+                    device_id_type=MESH,
+                )
             )
-        )
-        list_copies[-1].start()
+            list_copies[-1].start()
 
     def integrate(at, first):
         opac = opac_buf[at, pl.ds(first, ROWS)].reshape(height, share)
@@ -143,6 +144,18 @@
         return light, depth[(cells - 1) * ROWS :] * scale
 
     piece_copies = []
+    mine = pl.ds(pl.multiple_of(my_group * bricks, 2 * ROWS), bricks)
+
+    def send_piece(at):
+        return pltpu.make_async_remote_copy(
+            src_ref=piece.at[at],
+            dst_ref=table.at[:, :, mine, :],
+            send_sem=piece_send.at[at],
+            recv_sem=piece_recv.at[my_group],
+            device_id=(order[at], my_depth),
+            device_id_type=MESH,
+        )
+
     for at, peer in enumerate(order):
         loads[at][1].wait()
         loads[at][0].wait()
@@ -161,20 +174,15 @@
                     piece[at, c, 0, pl.ds(first, 2 * ROWS), at_lanes] = high[:, lanes]
                     piece[at, c, 1, pl.ds(first, 2 * ROWS), at_lanes] = low[:, lanes]
 
-        mine = pl.ds(pl.multiple_of(my_group * bricks, 2 * ROWS), bricks)
-        if at < n_group - 1:
-            copy = pltpu.make_async_remote_copy(
-                src_ref=piece.at[at],
-                dst_ref=table.at[:, :, mine, :],
-                send_sem=piece_send.at[at],
-                recv_sem=piece_recv.at[my_group],
-                device_id=(peer, my_depth),
-                device_id_type=MESH,
-            )
-            copy.start()
-            piece_copies.append(copy)
-        else:
-            table[:, :, mine, :] = piece[at]
+        if at + 1 == BEFORE:
+            enter()
+        if at + 1 >= BEFORE:
+            for done in range(at + 1 if at + 1 == BEFORE else 1):
+                done = done if at + 1 == BEFORE else at
+                if done < n_group - 1:
+                    piece_copies.append(send_piece(done))
+                    piece_copies[-1].start()
+    table[:, :, mine, :] = piece[n_group - 1]
 
     for at in range(n_group - 1):
         list_copies[at].wait_send()
@@ -272,10 +280,10 @@
         depth = depth + slab_depth
     for g in range(n_group):
         final[0, g * rows : (g + 1) * rows, :] = light[g]
-        final[1, g * rows : (g + 1) * rows, :] = jnp.exp(-depth[g])
+        final[1, g * rows : (g + 1) * rows, :] = depth[g]
     for i in range(steps):
-        image_out[i * sub : (i + 1) * sub, :] = final[0, pl.ds(i, sub, stride=steps), :]
-        trans_out[i * sub : (i + 1) * sub, :] = final[1, pl.ds(i, sub, stride=steps), :]
+        image_out[0, i * sub : (i + 1) * sub, :] = final[0, pl.ds(i, sub, stride=steps), :]
+        image_out[1, i * sub : (i + 1) * sub, :] = final[1, pl.ds(i, sub, stride=steps), :]
 
 
 def local(emission, opacity, brick_list, list_count):
@@ -289,11 +297,11 @@
     in_hbm = pl.BlockSpec(memory_space=pltpu.HBM)
     in_vmem = pl.BlockSpec(memory_space=pltpu.VMEM)
     dma = pltpu.SemaphoreType.DMA
-    image, trans = pl.pallas_call(
+    both = pl.pallas_call(
         functools.partial(kernel, n_group, n_depth, cells, slots, bricks, pixels, tiles),
-        out_shape=[jax.ShapeDtypeStruct((own, RAYS), jnp.float32)] * 2,
+        out_shape=jax.ShapeDtypeStruct((2, own, RAYS), jnp.float32),
         in_specs=[in_hbm] * 4,
-        out_specs=[in_vmem, in_vmem],
+        out_specs=in_vmem,
         scratch_shapes=[
             pltpu.VMEM((n_group, bricks, cells, share), jnp.bfloat16),
             pltpu.VMEM((n_group, bricks, cells, share), jnp.bfloat16),
@@ -317,10 +325,10 @@
             dma((n_depth, n_group)),
         ],
         compiler_params=pltpu.CompilerParams(
-            collective_id=0, has_side_effects=True, vmem_limit_bytes=60 * 1024 * 1024
+            collective_id=0, has_side_effects=True, vmem_limit_bytes=40000 * 1024
         ),
-    )(emission, opacity, jnp.swapaxes(brick_list, 1, 2), list_count)
-    return image, trans
+    )(pltpu.with_memory_space_constraint(emission, pltpu.HBM), pltpu.with_memory_space_constraint(opacity, pltpu.HBM), pltpu.with_memory_space_constraint(jnp.swapaxes(brick_list, 1, 2), pltpu.HBM), pltpu.with_memory_space_constraint(list_count, pltpu.HBM))
+    return both[0], jnp.exp(-both[1])
 
 
 def solution(mesh):

time: 24.9 us -> 21.7 us (0.87)
  local copies, waits for them, and re-layouts: 2.65 us -> 0 us
  Pallas kernels: 21.3 us -> 20.3 us
  other arithmetic: 0 us -> 0.62 us
    unnamed x2 -> x0, local copies, waits for them, and re-layouts: 2.65 us -> none
    pallas_call x1, Pallas kernels: 21.3 us -> 20.3 us  [local(): pl.pallas_call(functools.partial(kernel, n_group, n_depth, cells, slots,...]
    exp x0 -> x1, other arithmetic: none -> 0.62 us  [local(): return (both[0], jnp.exp(-both[1]))]
where the time goes in v3:
time: 21.7 us; the launch traced here: 21.5 us
  Pallas kernels  20.3 us (94%)
  between operations  0.64 us (3%)
  other arithmetic  0.62 us (3%)
    pallas_call x1, Pallas kernels, local(): pl.pallas_call(functools.partial(kernel, n_group, n_depth, cells, slots,...  20.3 us
    exp x1, other arithmetic, local(): return (both[0], jnp.exp(-both[1]))  0.62 us

profile of v3, /device:TPU:0, one launch (start us, length us, event | category | flops | bytes accessed | tf_op | source)
XLA Modules:
  0.0 21.5 jit_solution(10684928957639238408)
XLA Ops:
  0.6 20.3 %shard_map.59 = f32[2,32,128]{2,1,0:T(8,128)S(1)} custom-call(bf16[1,32,32,1024]{3,2,1,0:T(8,128)(2,1)} %emission.1, bf16[1,32,32,1024]{3,2,1,0:T(8,128)(2,1)} %opacity.1, s32[1,8,256]{2,1,0:T(8,128)} %bitcast.5, s32[1,256]{1,0:T(1,128)} %counts.1), custom_call_target="tpu_custom_call" | custom-call | tf_op jit(solution)/shard_map/pallas_call | solution.py:300
  20.9 0.6 %exponential_bitcast_fusion = (f32[32,128]{1,0:T(8,128)}, f32[32,128]{1,0:T(8,128)}) fusion(f32[2,32,128]{2,1,0:T(8,128)S(1)} %shard_map.59), kind=kLoop, calls=%fused_computation | loop fusion | flops 4096 | bytes 65536 | tf_op jit(solution)/shard_map/exp | solution.py:331

commit v4 on v3

--- a/solution.py
+++ b/solution.py
@@ -217,7 +217,7 @@
             src_ref=slab_buf.at[s, d],
             dst_ref=recv_buf.at[my_depth, my_group],
             send_sem=slab_send.at[s, d],
-            recv_sem=slab_recv.at[my_depth, my_group],
+            recv_sem=slab_recv,
             device_id=(s, d),
             device_id_type=MESH,
         )
@@ -253,7 +253,9 @@
             def _():
                 slab_copy(s, d).start()
 
-    recv_buf[my_depth, my_group] = slab_buf[my_group, my_depth]
+    pltpu.make_async_copy(
+        slab_buf.at[my_group, my_depth], recv_buf.at[my_depth, my_group], slab_recv
+    ).start()
 
     @pl.loop(0, n_group * n_depth)
     def _(which):
@@ -262,14 +264,8 @@
         @pl.when(jnp.logical_or(g != my_group, d != my_depth))
         def _():
             slab_copy(g, d).wait_send()
-            pltpu.make_async_remote_copy(
-                src_ref=slab_buf.at[g, d],
-                dst_ref=recv_buf.at[d, g],
-                send_sem=slab_send.at[g, d],
-                recv_sem=slab_recv.at[d, g],
-                device_id=(g, d),
-                device_id_type=MESH,
-            ).wait_recv()
+
+    pltpu.make_async_copy(recv_buf, recv_buf, slab_recv).wait()
 
     light = jnp.zeros((n_group, rows, RAYS), jnp.float32)
     depth = jnp.zeros((n_group, rows, RAYS), jnp.float32)
@@ -322,7 +318,7 @@
             dma((n_group,)),
             dma((n_group,)),
             dma((n_group, n_depth)),
-            dma((n_depth, n_group)),
+            dma(()),
         ],
         compiler_params=pltpu.CompilerParams(
             collective_id=0, has_side_effects=True, vmem_limit_bytes=40000 * 1024

time: 21.7 us -> 21.1 us (0.972)
  Pallas kernels: 20.3 us -> 19.6 us
    pallas_call x1, Pallas kernels: 20.3 us -> 19.6 us  [local(): pl.pallas_call(functools.partial(kernel, n_group, n_depth, cells, slots,...]
where the time goes in v4:
time: 21.1 us; the launch traced here: 20.9 us
  Pallas kernels  19.6 us (93%)
  between operations  0.64 us (3%)
  other arithmetic  0.62 us (3%)
    pallas_call x1, Pallas kernels, local(): pl.pallas_call(functools.partial(kernel, n_group, n_depth, cells, slots,...  19.6 us
    exp x1, other arithmetic, local(): return (both[0], jnp.exp(-both[1]))  0.62 us

profile of v4, /device:TPU:0, one launch (start us, length us, event | category | flops | bytes accessed | tf_op | source)
XLA Modules:
  0.0 20.9 jit_solution(7778377081691463368)
XLA Ops:
  0.6 19.6 %shard_map.59 = f32[2,32,128]{2,1,0:T(8,128)S(1)} custom-call(bf16[1,32,32,1024]{3,2,1,0:T(8,128)(2,1)} %emission.1, bf16[1,32,32,1024]{3,2,1,0:T(8,128)(2,1)} %opacity.1, s32[1,8,256]{2,1,0:T(8,128)} %bitcast.5, s32[1,256]{1,0:T(1,128)} %counts.1), custom_call_target="tpu_custom_call" | custom-call | tf_op jit(solution)/shard_map/pallas_call | solution.py:296
  20.3 0.6 %exponential_bitcast_fusion = (f32[32,128]{1,0:T(8,128)}, f32[32,128]{1,0:T(8,128)}) fusion(f32[2,32,128]{2,1,0:T(8,128)S(1)} %shard_map.59), kind=kLoop, calls=%fused_computation | loop fusion | flops 4096 | bytes 65536 | tf_op jit(solution)/shard_map/exp | solution.py:327
